TPU v7x, 128 devices: a whole 4x4x4 slice. The times are simulated.
128 devices in a mesh: row: 8 (over y, core), col: 16 (over x, z).
Axes of the slice: x: 4, y: 4, z: 4, core: 2. Of those that a mesh axis runs over, the one named last changes fastest.
Arguments:
- queries: bfloat16 [4, 16384, 256], P(None, ('row', 'col'))
- probes: int32 [4, 16384, 2], P(None, ('row', 'col')), may hold values from 0 to 127, all different within a row; in each aligned block of 128 rows (0 to 127, 128 to 255, ..., all dimensions but the last counted through in order) at most 4 rows name the same one
- keys: bfloat16 [128, 1024, 256], P(('row', 'col')), may hold values from -6 to 6
- values: bfloat16 [128, 1024, 256], P(('row', 'col')), may hold values from -6 to 6
- bucket_home: int32 [128], replicated, may hold values from 0 to 127, each once
- bucket_rows: int32 [128], replicated, may hold values from 1 to 1024, 49152 in all
Outputs:
- attended: bfloat16 [4, 16384, 256], P(None, ('row', 'col'))
Inputs may be any that keep to these rules, and one draw needn't show every extreme that they name: `probes`: each request names two different buckets; among the requests of one device in one step no bucket is named more than 4 times, a bound that some block reaches. `bucket_home`: each device holds exactly one bucket. `bucket_rows`: some bucket fills all 8 blocks.
All inputs are finite; a program needn't handle non-finite values.
Results may differ from a plain program's by a relative error of at most 0.007.
Values may be sent and summed in bfloat16 or wider, within the bound.
No kernel may reach another device: no remote copies, remote signals or barrier semaphores. Data moves between devices by JAX's collectives and lax.ppermute only.
A program may use at most 64 MiB of HBM per device.

v0:
```python
import math

import jax
import jax.numpy as jnp
from jax import lax
from jax.experimental import pallas as pl
from jax.experimental.pallas import tpu as pltpu
from jax.sharding import Mesh, PartitionSpec as P

H = 8
HD = 32
D = 256
KB = 256
QB = 256
SLOTS = 32
RET = 72
SCALE2 = math.log2(math.e) / math.sqrt(HD)
TINY = 2.0**-60
SAFE = 80.0
NORMS = (SAFE / SCALE2) ** 2 / 1.05

f32 = jnp.float32
bf16 = jnp.bfloat16
i32 = jnp.int32


def iota(shape, dim):
    return lax.broadcasted_iota(i32, shape, dim)


def dot(a, b):
    return jnp.dot(a, b, preferred_element_type=f32)


def dot_t(a, b):
    return lax.dot_general(a, b, (((1,), (1,)), ((), ())), preferred_element_type=f32)


def ones_where(cond):
    return jnp.where(cond, 1.0, 0.0).astype(bf16)


def pick_rows(index, shape):
    along = 1 if index.shape[1] == 1 else 0
    grid = iota(shape, along).astype(f32).astype(bf16)
    return jnp.where(grid == index.astype(bf16), jnp.ones(shape, bf16), jnp.zeros(shape, bf16))


def dispatch_kernel(probes_hbm, home_hbm, q_hbm, send_hbm, pos_ref, probes_ref, home_ref, q_ref, send_ref, in_sem, out_sem):
    copies = [
        pltpu.make_async_copy(source, target, in_sem.at[k])
        for k, (source, target) in enumerate(((home_hbm, home_ref), (probes_hbm, probes_ref), (q_hbm, q_ref)))
    ]
    for copy in copies:
        copy.start()
    steps = probes_ref.shape[0]
    n = 128
    tri = jnp.concatenate(
        [ones_where(iota((n, n), 0) < iota((n, n), 1)), jnp.ones((n, n), bf16)], axis=1
    )
    eye = iota((n, n), 0) == iota((n, n), 1)
    bucket = iota((n, n), 0)
    copies[0].wait()
    home_row = jnp.broadcast_to(home_ref[...].astype(f32), (n, n))
    home = dot(jnp.where(eye, home_row, 0.0).astype(bf16), jnp.ones((n, n), bf16)).astype(i32)
    core = (home >> 4) & 1
    chip = ((home >> 5) << 4) + (home & 15)
    base = (chip * SLOTS + core * 4).astype(f32)
    copies[1].wait()
    hits = [[bucket == probes_ref[t, j : j + 1, :] for j in range(2)] for t in range(steps)]
    counts = [[dot(ones_where(hit), tri) for hit in pair] for pair in hits]
    pos_rows = []
    for t in range(steps):
        before = base + 8.0 * t
        for j in range(2):
            mine = jnp.where(hits[t][j], counts[t][j][:, :n] + before, 0.0)
            pos_rows.append(jnp.sum(mine, axis=0, keepdims=True))
            before = before + counts[t][j][:, n:]
    pos = jnp.concatenate(pos_rows, axis=0)
    pos_ref[...] = pos
    rows = 256
    first = jnp.concatenate([pos[2 * t : 2 * t + 1] for t in range(steps)], axis=1)
    second = jnp.concatenate([pos[2 * t + 1 : 2 * t + 2] for t in range(steps)], axis=1)
    copies[2].wait()
    queries = q_ref[...].reshape(steps * n, D)
    lead = queries[:, :n]
    tiny = (iota((steps * n, n), 1) == 0) & (jnp.abs(lead.astype(f32)) < TINY)
    queries = jnp.concatenate([jnp.where(tiny, jnp.full(lead.shape, TINY, bf16), lead), queries[:, n:]], axis=1)
    chips = rows // SLOTS
    out_copies = []
    for block in range(send_ref.shape[0] // chips):
        pick = pick_rows(first - block * rows, (rows, steps * n)) + pick_rows(
            second - block * rows, (rows, steps * n)
        )
        out = dot(pick, queries).astype(bf16)
        part = pl.ds(block * chips, chips)
        send_ref[block * chips : (block + 1) * chips] = out.reshape(chips, SLOTS, D)
        out_copies.append(pltpu.make_async_copy(send_ref.at[part], send_hbm.at[part], out_sem.at[block]))
        out_copies[-1].start()
    for copy in out_copies:
        copy.wait()


def bucket_sizes(home_ref, rows_ref):
    core = lax.axis_index("core")
    columns = lax.axis_size("col")
    device = (lax.axis_index("y") * 2 + core) * columns + lax.axis_index("col")
    partner = device + columns * (1 - 2 * core)
    rows = rows_ref[...].astype(f32)

    def size(where):
        return jnp.sum(jnp.where(home_ref[...] == where, rows, 0.0)).astype(i32)

    return core, size(device), size(partner)


def prepare_kernel(home_ref, rows_ref, k_own, v_own, k_other, v_other, k_ref, vt_ref, valid_ref, stat_ref):
    _, own, other = bucket_sizes(home_ref, rows_ref)
    head_sum = ones_where((iota((D, 128), 0) // HD) == iota((D, 128), 1))
    for u in range(2):
        key_ref = (k_own, k_other)[u]
        value_ref = (v_own, v_other)[u]
        count = (own, other)[u]
        norm = jnp.zeros((KB, 128), f32)
        for kb in range(1024 // KB):
            key = key_ref[kb * KB : (kb + 1) * KB, :]
            k_ref[u, kb] = key
            norm = jnp.maximum(norm, dot(key * key, head_sum))
            valid = ones_where((iota((16, KB), 1) + kb * KB) < count)
            valid_ref[u, kb] = valid
            value = value_ref[kb * KB : (kb + 1) * KB, :]
            vt_ref[u, kb] = value.T * valid[0:1, :]
        stat_ref[u] = jnp.full((8, D), jnp.max(norm), f32)


def attention_kernel(
    home_ref, rows_ref, recv_ref, k_ref, vt_ref, valid_ref, stat_ref, ret_ref,
    qc_ref, oc_ref, qt_ref, p_ref, acc_ref, max_ref,
):
    n = 256
    half = n // 2
    srcs = n // SLOTS
    groups = recv_ref.shape[0] // srcs
    core, own, other = bucket_sizes(home_ref, rows_ref)

    def key_count(u):
        return jnp.where(u == 0, own, other)

    def slots(g):
        return recv_ref[srcs * g : srcs * (g + 1)].reshape(n, D)

    row = iota((groups, n), 0)
    side = (iota((1, n), 1) >> 2) & 1
    heads = ones_where((iota((16, D), 1) // HD) == iota((16, D), 0))
    norm = jnp.zeros((groups, n), f32)
    unsafe = jnp.zeros((8, n), f32)
    keys_norm = jnp.maximum(stat_ref[0, 0:1, :], stat_ref[1, 0:1, :])
    for g in range(groups):
        q = slots(g)
        squares = dot_t(heads, q * q)[0:8, :]
        unsafe = jnp.maximum(unsafe, jnp.where(squares * keys_norm <= NORMS, 0.0, 1.0))
        norm = jnp.where(row == g, jnp.sum(squares, axis=0, keepdims=True), norm)
    live = jnp.where(norm <= 0.0, 0.0, 1.0)
    side_in = (iota((n, n), 0) >> 2) & 1
    side_out = (iota((n, n), 1) >> 2) & 1
    upper = ones_where((iota((n, n), 0) < iota((n, n), 1)) & (side_in == side_out))
    rank = dot(live.astype(bf16), upper)
    code = jnp.where(live > 0.5, rank + (side * half).astype(f32), -1.0)
    code_t = code.T
    offsets = [[], []]
    ends = []
    for j in range(2):
        sizes = jnp.sum(jnp.where(side == j, live, 0.0), axis=1, keepdims=True).astype(i32)
        offset = jnp.int32(0)
        for g in range(groups):
            offsets[j].append(pl.multiple_of(offset, 16))
            offset = offset + ((sizes[g, 0] + 15) >> 4) * 16
        ends.append(offset)
    for g in range(groups):
        rows = dot(pick_rows(code[g : g + 1, :], (n, n)), slots(g)).astype(bf16)
        for j in range(2):
            qc_ref[j, pl.ds(offsets[j][g], half), :] = rows[j * half : (j + 1) * half]
    for j in range(2):
        after = pl.multiple_of(offsets[j][groups - 1] + half, 16)
        qc_ref[j, pl.ds(after, QB), :] = jnp.zeros((QB, D), bf16)
    fast = jnp.max(unsafe) < 0.5

    chunks = [(end + QB - 1) // QB for end in ends]
    blocks = [(key_count(j ^ core) + KB - 1) // KB for j in range(2)]

    def pick(j, pair):
        return jnp.where(j == 0, pair[0], pair[1])

    def queries_of(h):
        pieces = [
            qt_ref[h * HD : (h + 1) * HD, :] if k == h % 4 else jnp.zeros((HD, QB), bf16)
            for k in range(4)
        ]
        return jnp.concatenate(pieces, axis=0)

    def keys_of(u, kb, h):
        return k_ref[u, kb, :, (h // 4) * 128 : (h // 4 + 1) * 128]

    def finish(j, start, values, masses):
        count = values.shape[1]
        row = iota((8, count), 0)
        tiles = []
        for hh in range(4):
            low, high = masses(hh), masses(hh + 4)
            tile = jnp.zeros((8, count), f32)
            for k in range(len(low)):
                tile = jnp.where((row & 3) == k, jnp.where(row < 4, low[k], high[k]), tile)
            tiles.append(tile)
        wide = jnp.concatenate([values] + tiles * 4, axis=0).astype(bf16)
        turned = dot_t(ones_where(iota((count, count), 0) == iota((count, count), 1)), wide).astype(bf16)
        oc_ref[j, pl.ds(start, count), :] = turned

    def two(total):
        high = total.astype(bf16).astype(f32)
        return high, total - high

    def weights(u, kb, h):
        p_ref[h] = jnp.exp2(dot(keys_of(u, kb, h), queries_of(h)) * SCALE2).astype(bf16)

    def load_queries(j, ch):
        qt_ref[...] = qc_ref[j, pl.ds(pl.multiple_of(ch * QB, QB), QB), :].T

    def add_values(u, kb, h):
        lhs = jnp.concatenate([vt_ref[u, kb, h * HD : (h + 1) * HD, :], valid_ref[u, kb]], axis=0)
        acc_ref[h] += dot(lhs, p_ref[h])

    def fast_item(index, carry):
        j, ch, kb = carry
        ends_chunk = kb + 1 == pick(j, blocks)
        kb_next = jnp.where(ends_chunk, 0, kb + 1)
        ch_next = jnp.where(ends_chunk, ch + 1, ch)
        ends_bucket = ch_next == pick(j, chunks)
        ch_next = jnp.where(ends_bucket, 0, ch_next)
        j_next = jnp.minimum(jnp.where(ends_bucket, j + 1, j), 1)

        @pl.when(ends_chunk)
        def _():
            load_queries(j_next, ch_next)

        for h in range(0, H, 2):
            add_values(j ^ core, kb, h)
            add_values(j ^ core, kb, h + 1)
            weights(j_next ^ core, kb_next, h)
            weights(j_next ^ core, kb_next, h + 1)

        @pl.when(ends_chunk)
        def _():
            finish(
                j, pl.multiple_of(ch * QB, QB),
                jnp.concatenate([acc_ref[h, 0:HD, :] for h in range(H)], axis=0),
                lambda h: two(acc_ref[h, HD : HD + 8, :]),
            )
            acc_ref[...] = jnp.zeros(acc_ref.shape, f32)

        return j_next, ch_next, kb_next

    def slow_chunk(j, u, start, blocks, keys):
        acc_ref[...] = jnp.zeros(acc_ref.shape, f32)
        max_ref[...] = jnp.full(max_ref.shape, -3e38, f32)
        qt_ref[...] = qc_ref[j, pl.ds(start, QB), :].T

        def scores(kb, h):
            s = dot(keys_of(u, kb, h), queries_of(h)) * SCALE2
            return s, (iota((KB, QB), 0) + kb * KB) < keys

        def find(kb, carry):
            for h in range(H):
                s, valid = scores(kb, h)
                top = jnp.max(jnp.where(valid, s, -3e38), axis=0, keepdims=True)
                max_ref[h] = jnp.maximum(max_ref[h], top)
            return carry

        def block(kb, carry):
            for h in range(H):
                s, valid = scores(kb, h)
                p = jnp.where(valid, jnp.exp2(s - max_ref[h, 0:1, :]), 0.0).astype(bf16)
                lhs = jnp.concatenate([vt_ref[u, kb, h * HD : (h + 1) * HD, :], valid_ref[u, kb]], axis=0)
                acc_ref[h] += dot(lhs, p)
            return carry

        lax.fori_loop(0, blocks, find, 0)
        lax.fori_loop(0, blocks, block, 0)

        def masses(h):
            mass = jnp.log2(acc_ref[h, HD : HD + 8, :]) + max_ref[h]
            top, rest = two(mass)
            rest = rest.astype(bf16).astype(f32)
            return two(jnp.exp2(mass - top - rest)) + (top, rest)

        values = [acc_ref[h, 0:HD, :] / acc_ref[h, HD : HD + 1, :] for h in range(H)]
        finish(j, start, jnp.concatenate(values, axis=0), masses)

    @pl.when(fast)
    def _():
        start = jnp.where(chunks[0] > 0, 0, 1)
        load_queries(start, 0)
        acc_ref[...] = jnp.zeros(acc_ref.shape, f32)
        for h in range(H):
            weights(start ^ core, 0, h)
        total = chunks[0] * blocks[0] + chunks[1] * blocks[1]
        lax.fori_loop(0, total, fast_item, (start, jnp.int32(0), jnp.int32(0)))

    @pl.when(jnp.logical_not(fast))
    def _():
        def bucket(j, carry):
            def chunk(ch, carry):
                slow_chunk(j, j ^ core, pl.multiple_of(ch * QB, QB), pick(j, blocks), key_count(j ^ core))
                return carry

            return lax.fori_loop(0, pick(j, chunks), chunk, carry)

        lax.fori_loop(0, 2, bucket, 0)

    for j in range(2):
        done = pl.multiple_of(chunks[j] * QB, QB)
        oc_ref[j, pl.ds(done, half), :] = jnp.zeros((half, D + 128), bf16)

    own_lanes = (iota((8, 128), 1) >> 5) == (iota((8, 128), 0) & 3)
    own_lanes = jnp.concatenate([jnp.where(own_lanes, 1.0, 0.0)] * (n // 8), axis=0)
    mass_row = iota((8 * srcs, n), 0)
    mass_slot = iota((8 * srcs, n), 1)
    collect = ones_where(mass_row == (mass_slot >> 5) * 8 + ((mass_slot & 31) >> 2))

    def unpack(g):
        scatter = pick_rows(code_t[:, g : g + 1], (n, n))
        packed = jnp.concatenate([oc_ref[j, pl.ds(offsets[j][g], half), :] for j in range(2)], axis=0)
        return dot(scatter, packed)

    def write(g, rows):
        for k in range(2):
            out = rows[:, k * 128 : (k + 1) * 128].astype(bf16)
            ret_ref[srcs * g : srcs * (g + 1), k * SLOTS : (k + 1) * SLOTS, :] = out.reshape(srcs, SLOTS, 128)
        return (rows[:, D:] * own_lanes).astype(bf16)

    ahead = [unpack(g) for g in range(2)]
    spread = []
    for g in range(groups):
        if g + 2 < groups:
            ahead.append(unpack(g + 2))
        spread.append(write(g, ahead[g]))
    for g in range(groups):
        out = dot(collect, spread[g]).astype(bf16)
        ret_ref[srcs * g : srcs * (g + 1), 2 * SLOTS : 2 * SLOTS + 8, :] = out.reshape(srcs, 8, 128)


def combine_kernel(pos_ref, ret_ref, out_hbm, out_ref, out_sem):
    n = 128
    steps = out_ref.shape[0]
    chips = ret_ref.shape[0]
    pos = pos_ref[...].T
    lane_in = iota((n, D), 0) & 31
    head = iota((n, D), 1) // HD
    same_head = (lane_in >> 2) == 2 * (head & 3) + (head >> 2)
    widen = jnp.concatenate(
        [ones_where(same_head & ((lane_in & 3) < 2)), ones_where(same_head & ((lane_in & 3) >= 2))], axis=1
    )
    lane_slot = iota((2 * n, 128), 1) >> 5
    masses = ret_ref[:, 2 * SLOTS : 2 * SLOTS + 8, :].reshape(chips * 8, 128)
    copies = []
    lane = iota((2 * n, 128), 1)

    def gather(t):
        at = jnp.concatenate(
            [jnp.broadcast_to(pos[:, 2 * t + j : 2 * t + j + 1], (n, 128)) for j in range(2)], axis=0
        ).astype(i32)
        chip = at >> 5

        def pick(where):
            return jnp.concatenate([ones_where(lane == where - 128 * k) for k in range(chips * 8 // 128)], axis=1)

        values = pick(chip * 8 + (at & 7))
        values = [
            dot(values, ret_ref[:, k * SLOTS + 8 * t : k * SLOTS + 8 * t + 8, :].reshape(chips * 8, 128))
            for k in range(2)
        ]
        mass = dot(pick(chip * 8 + 2 * t + ((at >> 2) & 1)), masses)
        return jnp.concatenate(values, axis=1), jnp.where(lane_slot == (at & 3), mass, 0.0).astype(bf16)

    def merge(t, values, wide):
        total, top = wide[:, :D], wide[:, D:]
        highest = jnp.maximum(top[:n], top[n:])
        w0 = jnp.exp2(top[:n] - highest)
        w1 = jnp.exp2(top[n:] - highest)
        merged = (w0 * values[:n] + w1 * values[n:]) / (w0 * total[:n] + w1 * total[n:])
        out_ref[t] = merged.astype(bf16)
        copies.append(pltpu.make_async_copy(out_ref.at[t], out_hbm.at[t], out_sem.at[t]))
        copies[-1].start()

    ahead = [gather(0)]
    for t in range(steps):
        if t + 1 < steps:
            ahead.append(gather(t + 1))
        values, mass = ahead[t]
        merge(t, values, dot(mass, widen))
    for copy in copies:
        copy.wait()


def near(x):
    return pltpu.with_memory_space_constraint(x, pltpu.VMEM)


def hbm(x):
    return pltpu.with_memory_space_constraint(x, pltpu.HBM)


def call(kernel, name, mib, outs, args, scratch=()):
    spec = pl.BlockSpec(memory_space=pltpu.VMEM)
    single = not isinstance(outs, tuple)
    return pl.pallas_call(
        kernel,
        out_shape=outs,
        in_specs=[spec] * len(args),
        out_specs=spec if single else tuple(spec for _ in outs),
        scratch_shapes=list(scratch),
        compiler_params=pltpu.CompilerParams(vmem_limit_bytes=mib << 20),
        name=name,
    )(*args)


def body(queries, probes, keys, values, bucket_home, bucket_rows):
    chips = lax.axis_size("y") * lax.axis_size("col")
    steps = queries.shape[0]
    swap = [(0, 1), (1, 0)]
    k_own, v_own = keys[0], values[0]
    k_other = lax.ppermute(k_own, "core", swap)
    v_other = lax.ppermute(v_own, "core", swap)
    home = bucket_home.reshape(1, 128)
    rows = bucket_rows.reshape(1, 128)
    far = pl.BlockSpec(memory_space=pltpu.HBM)
    send, pos = pl.pallas_call(
        dispatch_kernel,
        out_shape=(jax.ShapeDtypeStruct((chips, SLOTS, D), bf16), pltpu.VMEM((2 * steps, 128), f32)),
        in_specs=[far] * 3,
        out_specs=(far, pl.BlockSpec(memory_space=pltpu.VMEM)),
        scratch_shapes=[
            pltpu.VMEM((steps, 2, 128), i32),
            pltpu.VMEM((1, 128), i32),
            pltpu.VMEM(queries.shape, bf16),
            pltpu.VMEM((chips, SLOTS, D), bf16),
            pltpu.SemaphoreType.DMA((3,)),
            pltpu.SemaphoreType.DMA((chips * SLOTS // 256,)),
        ],
        compiler_params=pltpu.CompilerParams(vmem_limit_bytes=16 << 20),
        name="dispatch",
    )(hbm(probes.transpose(0, 2, 1)), hbm(home), hbm(queries))
    recv = lax.all_to_all(send, ("y", "col"), split_axis=0, concat_axis=0, tiled=True)
    k, vt, valid, stat = call(
        prepare_kernel, "prepare", 16,
        (
            pltpu.VMEM((2, 4, KB, D), bf16),
            pltpu.VMEM((2, 4, D, KB), bf16),
            pltpu.VMEM((2, 4, 16, KB), bf16),
            pltpu.VMEM((2, 8, D), f32),
        ),
        (home, rows, hbm(k_own), hbm(v_own), k_other, v_other),
    )
    padded = chips * 16 + QB
    ret = call(
        attention_kernel, "attention", 24,
        pltpu.VMEM((chips, RET, 128), bf16),
        (home, rows, near(recv), near(k), near(vt), near(valid), near(stat)),
        (
            pltpu.VMEM((2, padded, D), bf16),
            pltpu.VMEM((2, padded, D + 128), bf16),
            pltpu.VMEM((D, QB), bf16),
            pltpu.VMEM((H, KB, QB), bf16),
            pltpu.VMEM((H, HD + 16, QB), f32),
            pltpu.VMEM((H, 8, QB), f32),
        ),
    )
    back = lax.all_to_all(ret, ("y", "col"), split_axis=0, concat_axis=0, tiled=True)
    return pl.pallas_call(
        combine_kernel,
        out_shape=jax.ShapeDtypeStruct(queries.shape, bf16),
        in_specs=[pl.BlockSpec(memory_space=pltpu.VMEM)] * 2,
        out_specs=far,
        scratch_shapes=[pltpu.VMEM(queries.shape, bf16), pltpu.SemaphoreType.DMA((steps,))],
        compiler_params=pltpu.CompilerParams(vmem_limit_bytes=24 << 20),
        name="combine",
    )(near(pos), near(back))


def solution(mesh):
    rows, columns = mesh.devices.shape
    split = Mesh(mesh.devices.reshape(rows // 2, 2, columns), ("y", "core", "col"))
    every = ("y", "core", "col")
    return jax.shard_map(
        body,
        mesh=split,
        in_specs=(
            P(None, every, None),
            P(None, every, None),
            P(every, None, None),
            P(every, None, None),
            P(),
            P(),
        ),
        out_specs=P(None, every, None),
        check_vma=False,
    )
```

profile of v0, /device:TPU:0, one launch (start us, length us, event | category | flops | bytes accessed | tf_op | source)
XLA Modules:
  0.0 110.5 jit_solution(10531754569018279319)
XLA Ops:
  0.0 0.0 copy-start.2
  0.0 0.0 copy-start.3
  0.0 0.0 copy-start
  0.0 0.0 copy-start.1
  0.0 2.7 %dispatch.1 = (bf16[64,32,256]{2,1,0:T(8,128)(2,1)}, f32[8,128]{1,0:T(8,128)S(1)}) custom-call(s32[4,2,128]{2,1,0:T(2,128)} %bitcast.14, s32[1,128]{1,0:T(1,128)} %bitcast.5, bf16[4,128,256]{2,1,0:T(8,128)(2,1)} %q_hbm.1), custom_call_target="tpu_custom_call" | custom-call | tf_op jit(solution)/shard_map/dispatch/pallas_call | solution.py:436
  2.7 11.5 %all-to-all-start = ((bf16[64,32,256]{2,1,0:T(8,128)(2,1)}), bf16[64,32,256]{2,1,0:T(8,128)(2,1)S(1)}, u32[]{:S(2)}, u32[]{:S(2)}) async-start(bf16[64,32,256]{2,1,0:T(8,128)(2,1)} %get-tuple-element.12), calls=%async_computation | async-start | bytes 2097152 | tf_op jit(solution)/shard_map/all_to_all | solution.py:452
  14.3 0.0 copy-done.2
  14.3 0.1 collective-permute-start
  14.4 0.0 copy-done.3
  14.4 0.5 collective-permute-start.1
  14.9 1.4 %collective-permute-done.k_other = bf16[1024,256]{1,0:T(8,128)(2,1)S(1)} collective-permute-done((bf16[1024,256]{1,0:T(8,128)(2,1)S(1)}, bf16[1024,256]{1,0:T(8,128)(2,1)S(1)}, u32[]{:S(2)}, u32[]{:S(2)}) %collective-permute-start) | collective-permute-done | bytes 524320 | tf_op jit(solution)/shard_map/ppermute | solution.py:431
  16.3 0.7 collective-permute-done.1.v_other
  17.0 0.0 copy-done
  17.0 0.0 copy-done.1
  17.0 1.9 %prepare.1 = (bf16[2,4,256,256]{3,2,1,0:T(8,128)(2,1)S(1)}, bf16[2,4,256,256]{3,2,1,0:T(8,128)(2,1)S(1)}, bf16[2,4,16,256]{3,2,1,0:T(8,128)(2,1)S(1)}, f32[2,8,256]{2,1,0:T(8,128)S(1)}) custom-call(s32[1,128]{1,0:T(1,128)S(1)} %bitcast.6, s32[1,128]{1,0:T(1,128)S(1)} %bitcast.8, bf16[1024,256]{1,0:T(8,128)(2,1)} %bitcast.10, bf16[1024,256]{1,0:T(8,128)(2,1)} %bitcast.12, ...), custom_call_target="tpu_custom_call" | custom-call | tf_op jit(solution)/shard_map/prepare/pallas_call | solution.py:415
  18.9 14.1 %all-to-all-done.recv_ref = bf16[64,32,256]{2,1,0:T(8,128)(2,1)S(1)} async-done(((bf16[64,32,256]{2,1,0:T(8,128)(2,1)}), bf16[64,32,256]{2,1,0:T(8,128)(2,1)S(1)}, u32[]{:S(2)}, u32[]{:S(2)}) %all-to-all-start) | async-done | bytes 1048608 | tf_op jit(solution)/shard_map/all_to_all | solution.py:452
  33.0 26.5 %attention.1 = bf16[64,72,128]{2,1,0:T(8,128)(2,1)S(1)} custom-call(s32[1,128]{1,0:T(1,128)S(1)} %bitcast.7, s32[1,128]{1,0:T(1,128)S(1)} %bitcast.9, bf16[64,32,256]{2,1,0:T(8,128)(2,1)S(1)} %all-to-all-done.recv_ref, bf16[2,4,256,256]{3,2,1,0:T(8,128)(2,1)S(1)} %get-tuple-element.13.k_ref, bf16[2,4,256,256]{3,2,1,0:T(8,128)(2,1)S(1)} %get-tuple-element.14.vt_ref, ...), custom_call_target="tpu_custom_call" | custom-call | tf_op jit(solution)/shard_map/attention/pallas_call | solution.py:415
  59.5 48.5 %all_to_all.10.ret_ref = bf16[64,72,128]{2,1,0:T(8,128)(2,1)S(1)} all-to-all(bf16[64,72,128]{2,1,0:T(8,128)(2,1)S(1)} %attention.1), channel_id=1, replica_groups=mesh['y'=4,'core'=2,'col'=16] {'y','col'}, dimensions={0} | all-to-all | bytes 2359296 | tf_op jit(solution)/shard_map/all_to_all | solution.py:477
  108.0 2.4 %combine.1 = bf16[4,128,256]{2,1,0:T(8,128)(2,1)} custom-call(f32[8,128]{1,0:T(8,128)S(1)} %get-tuple-element.11.pos_ref, bf16[64,72,128]{2,1,0:T(8,128)(2,1)S(1)} %all_to_all.10.ret_ref), custom_call_target="tpu_custom_call" | custom-call | tf_op jit(solution)/shard_map/combine/pallas_call | solution.py:478
Async XLA Ops:
  0.0 14.3 %copy-start.2 = (bf16[1,1024,256]{2,1,0:T(8,128)(2,1)S(1)}, bf16[1,1024,256]{2,1,0:T(8,128)(2,1)}, u32[]{:S(2)}) copy-start(bf16[1,1024,256]{2,1,0:T(8,128)(2,1)} %param.8) | copy-start | bytes 1572868
  0.0 14.4 %copy-start.3 = (bf16[1,1024,256]{2,1,0:T(8,128)(2,1)S(1)}, bf16[1,1024,256]{2,1,0:T(8,128)(2,1)}, u32[]{:S(2)}) copy-start(bf16[1,1024,256]{2,1,0:T(8,128)(2,1)} %param.9) | copy-start | bytes 1572868
  0.0 17.0 %copy-start = (s32[128]{0:T(128)S(1)}, s32[128]{0:T(128)}, u32[]{:S(2)}) copy-start(s32[128]{0:T(128)} %param.10) | copy-start | bytes 1540
  0.0 17.0 %copy-start.1 = (s32[128]{0:T(128)S(1)}, s32[128]{0:T(128)}, u32[]{:S(2)}) copy-start(s32[128]{0:T(128)} %param.11) | copy-start | bytes 1540
  2.7 30.3 %all-to-all-start = ((bf16[64,32,256]{2,1,0:T(8,128)(2,1)}), bf16[64,32,256]{2,1,0:T(8,128)(2,1)S(1)}, u32[]{:S(2)}, u32[]{:S(2)}) async-start(bf16[64,32,256]{2,1,0:T(8,128)(2,1)} %get-tuple-element.12), calls=%async_computation | async-start | bytes 2097152 | tf_op jit(solution)/shard_map/all_to_all | solution.py:452
  14.3 2.0 %collective-permute-start = (bf16[1024,256]{1,0:T(8,128)(2,1)S(1)}, bf16[1024,256]{1,0:T(8,128)(2,1)S(1)}, u32[]{:S(2)}, u32[]{:S(2)}) collective-permute-start(bf16[1024,256]{1,0:T(8,128)(2,1)S(1)} %bitcast.11), channel_id=1, source_target_pairs={{0,16},{16,0},{1,17},{17,1},{2,18},{18,2},{3,19},{19,3},{4,20},{20... | collective-permute-start | bytes 1572872 | tf_op jit(solution)/shard_map/ppermute | solution.py:431
  14.4 2.6 %collective-permute-start.1 = (bf16[1024,256]{1,0:T(8,128)(2,1)S(1)}, bf16[1024,256]{1,0:T(8,128)(2,1)S(1)}, u32[]{:S(2)}, u32[]{:S(2)}) collective-permute-start(bf16[1024,256]{1,0:T(8,128)(2,1)S(1)} %bitcast.13), channel_id=1, source_target_pairs={{0,16},{16,0},{1,17},{17,1},{2,18},{18,2},{3,19},{19,3},{4,20},{20... | collective-permute-start | bytes 1572872 | tf_op jit(solution)/shard_map/ppermute | solution.py:432
where the time goes:
time: 110 us
  blocking collectives  48.5 us (44%)
  Pallas kernels  33.6 us (31%)
  waiting for transfers between devices  16.2 us (15%)
  starting transfers between devices  12.1 us (11%)
    all_to_all x1, blocking collectives, body(): lax.all_to_all(ret, ('y', 'col'), split_axis=0, concat_axis=0, tiled=True)  48.5 us
    pallas_call x2, Pallas kernels, call(): pl.pallas_call(kernel, out_shape=outs, in_specs=[spec] * len(args), out_s...  28.4 us
    all_to_all x1, waiting for transfers between devices, body(): lax.all_to_all(send, ('y', 'col'), split_axis=0, concat_axis=0, tiled=True)  14.1 us
    all_to_all x1, starting transfers between devices, body(): lax.all_to_all(send, ('y', 'col'), split_axis=0, concat_axis=0, tiled=True)  11.5 us
    pallas_call x1, Pallas kernels, body(): pl.pallas_call(dispatch_kernel, out_shape=(jax.ShapeDtypeStruct((chips, S...  2.72 us
    pallas_call x1, Pallas kernels, body(): pl.pallas_call(combine_kernel, out_shape=jax.ShapeDtypeStruct(queries.sha...  2.44 us
  transfers between devices with their start and end apart: 3, of which 3 were waited for; matrix products, arithmetic and copies ran while one was open for 0% of the time, Pallas kernels for 2%

commit v1 on v0

--- a/solution.py
+++ b/solution.py
@@ -12,6 +12,7 @@
 D = 256
 KB = 256
 QB = 256
+EARLY = 4
 SLOTS = 32
 RET = 72
 SCALE2 = math.log2(math.e) / math.sqrt(HD)
@@ -65,13 +66,13 @@
     home = dot(jnp.where(eye, home_row, 0.0).astype(bf16), jnp.ones((n, n), bf16)).astype(i32)
     core = (home >> 4) & 1
     chip = ((home >> 5) << 4) + (home & 15)
-    base = (chip * SLOTS + core * 4).astype(f32)
+    base = (chip * 8 + core * 4).astype(f32)
     copies[1].wait()
     hits = [[bucket == probes_ref[t, j : j + 1, :] for j in range(2)] for t in range(steps)]
     counts = [[dot(ones_where(hit), tri) for hit in pair] for pair in hits]
     pos_rows = []
     for t in range(steps):
-        before = base + 8.0 * t
+        before = base
         for j in range(2):
             mine = jnp.where(hits[t][j], counts[t][j][:, :n] + before, 0.0)
             pos_rows.append(jnp.sum(mine, axis=0, keepdims=True))
@@ -79,23 +80,19 @@
     pos = jnp.concatenate(pos_rows, axis=0)
     pos_ref[...] = pos
     rows = 256
-    first = jnp.concatenate([pos[2 * t : 2 * t + 1] for t in range(steps)], axis=1)
-    second = jnp.concatenate([pos[2 * t + 1 : 2 * t + 2] for t in range(steps)], axis=1)
+    chips = rows // 8
     copies[2].wait()
-    queries = q_ref[...].reshape(steps * n, D)
-    lead = queries[:, :n]
-    tiny = (iota((steps * n, n), 1) == 0) & (jnp.abs(lead.astype(f32)) < TINY)
-    queries = jnp.concatenate([jnp.where(tiny, jnp.full(lead.shape, TINY, bf16), lead), queries[:, n:]], axis=1)
-    chips = rows // SLOTS
     out_copies = []
-    for block in range(send_ref.shape[0] // chips):
-        pick = pick_rows(first - block * rows, (rows, steps * n)) + pick_rows(
-            second - block * rows, (rows, steps * n)
-        )
-        out = dot(pick, queries).astype(bf16)
-        part = pl.ds(block * chips, chips)
-        send_ref[block * chips : (block + 1) * chips] = out.reshape(chips, SLOTS, D)
-        out_copies.append(pltpu.make_async_copy(send_ref.at[part], send_hbm.at[part], out_sem.at[block]))
+    for t in range(steps):
+        lead = q_ref[t, :, :n]
+        tiny = (iota((n, n), 1) == 0) & (jnp.abs(lead.astype(f32)) < TINY)
+        queries = jnp.concatenate([jnp.where(tiny, jnp.full(lead.shape, TINY, bf16), lead), q_ref[t, :, n:]], axis=1)
+        for block in range(send_ref.shape[0] // chips):
+            pick = sum(pick_rows(pos[2 * t + j : 2 * t + j + 1] - block * rows, (rows, n)) for j in range(2))
+            out = dot(pick, queries).astype(bf16)
+            send_ref[block * chips : (block + 1) * chips, 8 * t : 8 * t + 8, :] = out.reshape(chips, 8, D)
+        part = pl.ds(8 * t, 8)
+        out_copies.append(pltpu.make_async_copy(send_ref.at[:, part, :], send_hbm.at[:, part, :], out_sem.at[t]))
         out_copies[-1].start()
     for copy in out_copies:
         copy.wait()
@@ -135,7 +132,7 @@
 
 def attention_kernel(
     home_ref, rows_ref, recv_ref, k_ref, vt_ref, valid_ref, stat_ref, ret_ref,
-    qc_ref, oc_ref, qt_ref, p_ref, acc_ref, max_ref,
+    qc_ref, oc_ref, qt_ref, late_ref, p_ref, acc_ref, max_ref,
 ):
     n = 256
     half = n // 2
@@ -219,8 +216,12 @@
         high = total.astype(bf16).astype(f32)
         return high, total - high
 
-    def weights(u, kb, h):
-        p_ref[h] = jnp.exp2(dot(keys_of(u, kb, h), queries_of(h)) * SCALE2).astype(bf16)
+    def weights(u, kb, h, queries):
+        p_ref[h] = jnp.exp2(dot(keys_of(u, kb, h), queries) * SCALE2).astype(bf16)
+
+    def late_queries_of(h):
+        part = late_ref[(h - EARLY) * HD : (h - EARLY + 1) * HD, :]
+        return jnp.concatenate([part if k == h % 4 else jnp.zeros((HD, QB), bf16) for k in range(4)], axis=0)
 
     def load_queries(j, ch):
         qt_ref[...] = qc_ref[j, pl.ds(pl.multiple_of(ch * QB, QB), QB), :].T
@@ -238,15 +239,25 @@
         ch_next = jnp.where(ends_bucket, 0, ch_next)
         j_next = jnp.minimum(jnp.where(ends_bucket, j + 1, j), 1)
 
+        @pl.when(kb == 0)
+        def _():
+            late_ref[...] = qt_ref[EARLY * HD :, :]
+
         @pl.when(ends_chunk)
         def _():
             load_queries(j_next, ch_next)
 
-        for h in range(0, H, 2):
-            add_values(j ^ core, kb, h)
-            add_values(j ^ core, kb, h + 1)
-            weights(j_next ^ core, kb_next, h)
-            weights(j_next ^ core, kb_next, h + 1)
+        u, u_next = j ^ core, j_next ^ core
+        for h in range(EARLY, H):
+            weights(u, kb, h, late_queries_of(h))
+        add_values(u, kb, 0)
+        add_values(u, kb, 1)
+        for h in range(EARLY):
+            weights(u_next, kb_next, h, queries_of(h))
+            if h + 2 < EARLY:
+                add_values(u, kb, h + 2)
+        for h in range(EARLY, H):
+            add_values(u, kb, h)
 
         @pl.when(ends_chunk)
         def _():
@@ -300,8 +311,8 @@
         start = jnp.where(chunks[0] > 0, 0, 1)
         load_queries(start, 0)
         acc_ref[...] = jnp.zeros(acc_ref.shape, f32)
-        for h in range(H):
-            weights(start ^ core, 0, h)
+        for h in range(EARLY):
+            weights(start ^ core, 0, h, queries_of(h))
         total = chunks[0] * blocks[0] + chunks[1] * blocks[1]
         lax.fori_loop(0, total, fast_item, (start, jnp.int32(0), jnp.int32(0)))
 
@@ -352,34 +363,39 @@
     n = 128
     steps = out_ref.shape[0]
     chips = ret_ref.shape[0]
-    pos = pos_ref[...].T
     lane_in = iota((n, D), 0) & 31
     head = iota((n, D), 1) // HD
     same_head = (lane_in >> 2) == 2 * (head & 3) + (head >> 2)
     widen = jnp.concatenate(
         [ones_where(same_head & ((lane_in & 3) < 2)), ones_where(same_head & ((lane_in & 3) >= 2))], axis=1
     )
-    lane_slot = iota((2 * n, 128), 1) >> 5
+    at = pos_ref[...].astype(i32)
+    step = iota(at.shape, 0) >> 1
+    columns = []
+    for row in (at, (at & -8) + 2 * step + ((at >> 2) & 1)):
+        columns += [jnp.where(row < 256, row, -1), jnp.where(row < 256, -1, row - 256)]
+    columns = jnp.concatenate(columns + [at & 3], axis=0).astype(f32).T
+    lane_slot = (iota((2 * n, n), 1) >> 5).astype(f32).astype(bf16)
+    lanes = [(iota((2 * n, n), 1) + n * k).astype(f32).astype(bf16) for k in range(2)]
+    one, zero = jnp.ones((2 * n, n), bf16), jnp.zeros((2 * n, n), bf16)
     masses = ret_ref[:, 2 * SLOTS : 2 * SLOTS + 8, :].reshape(chips * 8, 128)
     copies = []
-    lane = iota((2 * n, 128), 1)
 
     def gather(t):
-        at = jnp.concatenate(
-            [jnp.broadcast_to(pos[:, 2 * t + j : 2 * t + j + 1], (n, 128)) for j in range(2)], axis=0
-        ).astype(i32)
-        chip = at >> 5
-
-        def pick(where):
-            return jnp.concatenate([ones_where(lane == where - 128 * k) for k in range(chips * 8 // 128)], axis=1)
-
-        values = pick(chip * 8 + (at & 7))
-        values = [
-            dot(values, ret_ref[:, k * SLOTS + 8 * t : k * SLOTS + 8 * t + 8, :].reshape(chips * 8, 128))
-            for k in range(2)
-        ]
-        mass = dot(pick(chip * 8 + 2 * t + ((at >> 2) & 1)), masses)
-        return jnp.concatenate(values, axis=1), jnp.where(lane_slot == (at & 3), mass, 0.0).astype(bf16)
+        def column(k):
+            first = 8 * k + 2 * t
+            both = [jnp.broadcast_to(columns[:, c : c + 1], (n, n)) for c in (first, first + 1)]
+            return jnp.concatenate(both, axis=0).astype(bf16)
+
+        def pick(k):
+            return jnp.concatenate(
+                [jnp.where(column(k + side) == lane, one, zero) for side in range(2) for lane in lanes], axis=1
+            )
+
+        rows = [ret_ref[:, k * SLOTS + 8 * t : k * SLOTS + 8 * t + 8, :].reshape(chips * 8, 128) for k in range(2)]
+        values = dot(pick(0), jnp.concatenate(rows, axis=1))
+        mass = dot(pick(2), masses).astype(bf16)
+        return values, jnp.where(column(4) == lane_slot, mass, zero)
 
     def merge(t, values, wide):
         total, top = wide[:, :D], wide[:, D:]
@@ -444,7 +460,7 @@
             pltpu.VMEM(queries.shape, bf16),
             pltpu.VMEM((chips, SLOTS, D), bf16),
             pltpu.SemaphoreType.DMA((3,)),
-            pltpu.SemaphoreType.DMA((chips * SLOTS // 256,)),
+            pltpu.SemaphoreType.DMA((steps,)),
         ],
         compiler_params=pltpu.CompilerParams(vmem_limit_bytes=16 << 20),
         name="dispatch",
@@ -469,6 +485,7 @@
             pltpu.VMEM((2, padded, D), bf16),
             pltpu.VMEM((2, padded, D + 128), bf16),
             pltpu.VMEM((D, QB), bf16),
+            pltpu.VMEM(((H - EARLY) * HD, QB), bf16),
             pltpu.VMEM((H, KB, QB), bf16),
             pltpu.VMEM((H, HD + 16, QB), f32),
             pltpu.VMEM((H, 8, QB), f32),

time: 110 us -> 109 us (level); the launches traced: 110 us -> 108 us
  Pallas kernels: 33.6 us -> 25.7 us
  blocking collectives: 48.5 us -> 54.1 us
    pallas_call x2, Pallas kernels: 28.4 us -> 21.3 us  [call(): pl.pallas_call(kernel, out_shape=outs, in_specs=[spec] * len(args), out_s...]
    all_to_all x1, blocking collectives: 48.5 us -> 54.1 us  [body(): lax.all_to_all(ret, ('y', 'col'), split_axis=0, concat_axis=0, tiled=True)]
where the time goes in v1:
time: 109 us; the launch traced here: 108 us
  blocking collectives  54.1 us (50%)
  Pallas kernels  25.7 us (24%)
  waiting for transfers between devices  16.2 us (15%)
  starting transfers between devices  12.1 us (11%)
    all_to_all x1, blocking collectives, body(): lax.all_to_all(ret, ('y', 'col'), split_axis=0, concat_axis=0, tiled=True)  54.1 us
    pallas_call x2, Pallas kernels, call(): pl.pallas_call(kernel, out_shape=outs, in_specs=[spec] * len(args), out_s...  21.3 us
    all_to_all x1, waiting for transfers between devices, body(): lax.all_to_all(send, ('y', 'col'), split_axis=0, concat_axis=0, tiled=True)  14.1 us
    all_to_all x1, starting transfers between devices, body(): lax.all_to_all(send, ('y', 'col'), split_axis=0, concat_axis=0, tiled=True)  11.5 us
    pallas_call x1, Pallas kernels, body(): pl.pallas_call(dispatch_kernel, out_shape=(jax.ShapeDtypeStruct((chips, S...  2.52 us
  transfers between devices with their start and end apart: 3, of which 3 were waited for; matrix products, arithmetic and copies ran while one was open for 0% of the time, Pallas kernels for 2%

profile of v1, /device:TPU:0, one launch (start us, length us, event | category | flops | bytes accessed | tf_op | source)
XLA Modules:
  0.0 108.2 jit_solution(10617940695673338360)
XLA Ops:
  0.0 0.0 copy-start.2
  0.0 0.0 copy-start.3
  0.0 0.0 copy-start
  0.0 0.0 copy-start.1
  0.0 2.5 %dispatch.1 = (bf16[64,32,256]{2,1,0:T(8,128)(2,1)}, f32[8,128]{1,0:T(8,128)S(1)}) custom-call(s32[4,2,128]{2,1,0:T(2,128)} %bitcast.14, s32[1,128]{1,0:T(1,128)} %bitcast.5, bf16[4,128,256]{2,1,0:T(8,128)(2,1)} %q_hbm.1), custom_call_target="tpu_custom_call" | custom-call | tf_op jit(solution)/shard_map/dispatch/pallas_call | solution.py:452
  2.5 11.5 %all-to-all-start = ((bf16[64,32,256]{2,1,0:T(8,128)(2,1)}), bf16[64,32,256]{2,1,0:T(8,128)(2,1)S(1)}, u32[]{:S(2)}, u32[]{:S(2)}) async-start(bf16[64,32,256]{2,1,0:T(8,128)(2,1)} %get-tuple-element.12), calls=%async_computation | async-start | bytes 2097152 | tf_op jit(solution)/shard_map/all_to_all | solution.py:468
  14.1 0.0 copy-done.2
  14.1 0.1 collective-permute-start
  14.2 0.0 copy-done.3
  14.2 0.5 collective-permute-start.1
  14.7 1.4 %collective-permute-done.k_other = bf16[1024,256]{1,0:T(8,128)(2,1)S(1)} collective-permute-done((bf16[1024,256]{1,0:T(8,128)(2,1)S(1)}, bf16[1024,256]{1,0:T(8,128)(2,1)S(1)}, u32[]{:S(2)}, u32[]{:S(2)}) %collective-permute-start) | collective-permute-done | bytes 524320 | tf_op jit(solution)/shard_map/ppermute | solution.py:447
  16.1 0.7 collective-permute-done.1.v_other
  16.8 0.0 copy-done
  16.8 0.0 copy-done.1
  16.8 1.9 %prepare.1 = (bf16[2,4,256,256]{3,2,1,0:T(8,128)(2,1)S(1)}, bf16[2,4,256,256]{3,2,1,0:T(8,128)(2,1)S(1)}, bf16[2,4,16,256]{3,2,1,0:T(8,128)(2,1)S(1)}, f32[2,8,256]{2,1,0:T(8,128)S(1)}) custom-call(s32[1,128]{1,0:T(1,128)S(1)} %bitcast.6, s32[1,128]{1,0:T(1,128)S(1)} %bitcast.8, bf16[1024,256]{1,0:T(8,128)(2,1)} %bitcast.10, bf16[1024,256]{1,0:T(8,128)(2,1)} %bitcast.12, ...), custom_call_target="tpu_custom_call" | custom-call | tf_op jit(solution)/shard_map/prepare/pallas_call | solution.py:431
  18.7 14.1 %all-to-all-done.recv_ref = bf16[64,32,256]{2,1,0:T(8,128)(2,1)S(1)} async-done(((bf16[64,32,256]{2,1,0:T(8,128)(2,1)}), bf16[64,32,256]{2,1,0:T(8,128)(2,1)S(1)}, u32[]{:S(2)}, u32[]{:S(2)}) %all-to-all-start) | async-done | bytes 1048608 | tf_op jit(solution)/shard_map/all_to_all | solution.py:468
  32.8 19.4 %attention.1 = bf16[64,72,128]{2,1,0:T(8,128)(2,1)S(1)} custom-call(s32[1,128]{1,0:T(1,128)S(1)} %bitcast.7, s32[1,128]{1,0:T(1,128)S(1)} %bitcast.9, bf16[64,32,256]{2,1,0:T(8,128)(2,1)S(1)} %all-to-all-done.recv_ref, bf16[2,4,256,256]{3,2,1,0:T(8,128)(2,1)S(1)} %get-tuple-element.13.k_ref, bf16[2,4,256,256]{3,2,1,0:T(8,128)(2,1)S(1)} %get-tuple-element.14.vt_ref, ...), custom_call_target="tpu_custom_call" | custom-call | tf_op jit(solution)/shard_map/attention/pallas_call | solution.py:431
  52.2 54.1 %all_to_all.10.ret_ref = bf16[64,72,128]{2,1,0:T(8,128)(2,1)S(1)} all-to-all(bf16[64,72,128]{2,1,0:T(8,128)(2,1)S(1)} %attention.1), channel_id=1, replica_groups=mesh['y'=4,'core'=2,'col'=16] {'y','col'}, dimensions={0} | all-to-all | bytes 2359296 | tf_op jit(solution)/shard_map/all_to_all | solution.py:494
  106.4 1.9 %combine.1 = bf16[4,128,256]{2,1,0:T(8,128)(2,1)} custom-call(f32[8,128]{1,0:T(8,128)S(1)} %get-tuple-element.11.pos_ref, bf16[64,72,128]{2,1,0:T(8,128)(2,1)S(1)} %all_to_all.10.ret_ref), custom_call_target="tpu_custom_call" | custom-call | tf_op jit(solution)/shard_map/combine/pallas_call | solution.py:495
Async XLA Ops:
  0.0 14.1 %copy-start.2 = (bf16[1,1024,256]{2,1,0:T(8,128)(2,1)S(1)}, bf16[1,1024,256]{2,1,0:T(8,128)(2,1)}, u32[]{:S(2)}) copy-start(bf16[1,1024,256]{2,1,0:T(8,128)(2,1)} %param.8) | copy-start | bytes 1572868
  0.0 14.2 %copy-start.3 = (bf16[1,1024,256]{2,1,0:T(8,128)(2,1)S(1)}, bf16[1,1024,256]{2,1,0:T(8,128)(2,1)}, u32[]{:S(2)}) copy-start(bf16[1,1024,256]{2,1,0:T(8,128)(2,1)} %param.9) | copy-start | bytes 1572868
  0.0 16.8 %copy-start = (s32[128]{0:T(128)S(1)}, s32[128]{0:T(128)}, u32[]{:S(2)}) copy-start(s32[128]{0:T(128)} %param.10) | copy-start | bytes 1540
  0.0 16.8 %copy-start.1 = (s32[128]{0:T(128)S(1)}, s32[128]{0:T(128)}, u32[]{:S(2)}) copy-start(s32[128]{0:T(128)} %param.11) | copy-start | bytes 1540
  2.5 30.3 %all-to-all-start = ((bf16[64,32,256]{2,1,0:T(8,128)(2,1)}), bf16[64,32,256]{2,1,0:T(8,128)(2,1)S(1)}, u32[]{:S(2)}, u32[]{:S(2)}) async-start(bf16[64,32,256]{2,1,0:T(8,128)(2,1)} %get-tuple-element.12), calls=%async_computation | async-start | bytes 2097152 | tf_op jit(solution)/shard_map/all_to_all | solution.py:468
  14.1 2.0 %collective-permute-start = (bf16[1024,256]{1,0:T(8,128)(2,1)S(1)}, bf16[1024,256]{1,0:T(8,128)(2,1)S(1)}, u32[]{:S(2)}, u32[]{:S(2)}) collective-permute-start(bf16[1024,256]{1,0:T(8,128)(2,1)S(1)} %bitcast.11), channel_id=1, source_target_pairs={{0,16},{16,0},{1,17},{17,1},{2,18},{18,2},{3,19},{19,3},{4,20},{20... | collective-permute-start | bytes 1572872 | tf_op jit(solution)/shard_map/ppermute | solution.py:447
  14.2 2.6 %collective-permute-start.1 = (bf16[1024,256]{1,0:T(8,128)(2,1)S(1)}, bf16[1024,256]{1,0:T(8,128)(2,1)S(1)}, u32[]{:S(2)}, u32[]{:S(2)}) collective-permute-start(bf16[1024,256]{1,0:T(8,128)(2,1)S(1)} %bitcast.13), channel_id=1, source_target_pairs={{0,16},{16,0},{1,17},{17,1},{2,18},{18,2},{3,19},{19,3},{4,20},{20... | collective-permute-start | bytes 1572872 | tf_op jit(solution)/shard_map/ppermute | solution.py:448

commit v2 on v1

--- a/solution.py
+++ b/solution.py
@@ -209,8 +209,7 @@
                 tile = jnp.where((row & 3) == k, jnp.where(row < 4, low[k], high[k]), tile)
             tiles.append(tile)
         wide = jnp.concatenate([values] + tiles * 4, axis=0).astype(bf16)
-        turned = dot_t(ones_where(iota((count, count), 0) == iota((count, count), 1)), wide).astype(bf16)
-        oc_ref[j, pl.ds(start, count), :] = turned
+        oc_ref[j, pl.ds(start, count), :] = wide.T
 
     def two(total):
         high = total.astype(bf16).astype(f32)
@@ -226,9 +225,9 @@
     def load_queries(j, ch):
         qt_ref[...] = qc_ref[j, pl.ds(pl.multiple_of(ch * QB, QB), QB), :].T
 
-    def add_values(u, kb, h):
+    def add_values(u, kb, h, keep):
         lhs = jnp.concatenate([vt_ref[u, kb, h * HD : (h + 1) * HD, :], valid_ref[u, kb]], axis=0)
-        acc_ref[h] += dot(lhs, p_ref[h])
+        acc_ref[h] = acc_ref[h] * keep + dot(lhs, p_ref[h])
 
     def fast_item(index, carry):
         j, ch, kb = carry
@@ -248,16 +247,17 @@
             load_queries(j_next, ch_next)
 
         u, u_next = j ^ core, j_next ^ core
+        keep = jnp.where(kb == 0, 0.0, 1.0)
         for h in range(EARLY, H):
             weights(u, kb, h, late_queries_of(h))
-        add_values(u, kb, 0)
-        add_values(u, kb, 1)
+        add_values(u, kb, 0, keep)
+        add_values(u, kb, 1, keep)
         for h in range(EARLY):
             weights(u_next, kb_next, h, queries_of(h))
             if h + 2 < EARLY:
-                add_values(u, kb, h + 2)
+                add_values(u, kb, h + 2, keep)
         for h in range(EARLY, H):
-            add_values(u, kb, h)
+            add_values(u, kb, h, keep)
 
         @pl.when(ends_chunk)
         def _():
@@ -266,7 +266,6 @@
                 jnp.concatenate([acc_ref[h, 0:HD, :] for h in range(H)], axis=0),
                 lambda h: two(acc_ref[h, HD : HD + 8, :]),
             )
-            acc_ref[...] = jnp.zeros(acc_ref.shape, f32)
 
         return j_next, ch_next, kb_next
 

time: 109 us -> 107 us (0.982); the launches traced: 108 us -> 108 us
  Pallas kernels: 25.7 us -> 41.8 us
  blocking collectives: 54.1 us -> 38.1 us
    pallas_call x2, Pallas kernels: 21.3 us -> 37.4 us  [call(): pl.pallas_call(kernel, out_shape=outs, in_specs=[spec] * len(args), out_s...]
    all_to_all x1, blocking collectives: 54.1 us -> 38.1 us  [body(): lax.all_to_all(ret, ('y', 'col'), split_axis=0, concat_axis=0, tiled=True)]
where the time goes in v2:
time: 107 us; the launch traced here: 108 us
  Pallas kernels  41.8 us (39%)
  blocking collectives  38.1 us (36%)
  waiting for transfers between devices  16.2 us (15%)
  starting transfers between devices  12.1 us (11%)
    all_to_all x1, blocking collectives, body(): lax.all_to_all(ret, ('y', 'col'), split_axis=0, concat_axis=0, tiled=True)  38.1 us
    pallas_call x2, Pallas kernels, call(): pl.pallas_call(kernel, out_shape=outs, in_specs=[spec] * len(args), out_s...  37.4 us
    all_to_all x1, waiting for transfers between devices, body(): lax.all_to_all(send, ('y', 'col'), split_axis=0, concat_axis=0, tiled=True)  14.1 us
    all_to_all x1, starting transfers between devices, body(): lax.all_to_all(send, ('y', 'col'), split_axis=0, concat_axis=0, tiled=True)  11.5 us
    pallas_call x1, Pallas kernels, body(): pl.pallas_call(dispatch_kernel, out_shape=(jax.ShapeDtypeStruct((chips, S...  2.52 us
  transfers between devices with their start and end apart: 3, of which 3 were waited for; matrix products, arithmetic and copies ran while one was open for 0% of the time, Pallas kernels for 2%

profile of v2, /device:TPU:0, one launch (start us, length us, event | category | flops | bytes accessed | tf_op | source)
XLA Modules:
  0.0 108.3 jit_solution(8639523551225469536)
XLA Ops:
  0.0 0.0 copy-start.2
  0.0 0.0 copy-start.3
  0.0 0.0 copy-start
  0.0 0.0 copy-start.1
  0.0 2.5 %dispatch.1 = (bf16[64,32,256]{2,1,0:T(8,128)(2,1)}, f32[8,128]{1,0:T(8,128)S(1)}) custom-call(s32[4,2,128]{2,1,0:T(2,128)} %bitcast.14, s32[1,128]{1,0:T(1,128)} %bitcast.5, bf16[4,128,256]{2,1,0:T(8,128)(2,1)} %q_hbm.1), custom_call_target="tpu_custom_call" | custom-call | tf_op jit(solution)/shard_map/dispatch/pallas_call | solution.py:451
  2.5 11.5 %all-to-all-start = ((bf16[64,32,256]{2,1,0:T(8,128)(2,1)}), bf16[64,32,256]{2,1,0:T(8,128)(2,1)S(1)}, u32[]{:S(2)}, u32[]{:S(2)}) async-start(bf16[64,32,256]{2,1,0:T(8,128)(2,1)} %get-tuple-element.12), calls=%async_computation | async-start | bytes 2097152 | tf_op jit(solution)/shard_map/all_to_all | solution.py:467
  14.1 0.0 copy-done.2
  14.1 0.1 collective-permute-start
  14.2 0.0 copy-done.3
  14.2 0.5 collective-permute-start.1
  14.7 1.4 %collective-permute-done.k_other = bf16[1024,256]{1,0:T(8,128)(2,1)S(1)} collective-permute-done((bf16[1024,256]{1,0:T(8,128)(2,1)S(1)}, bf16[1024,256]{1,0:T(8,128)(2,1)S(1)}, u32[]{:S(2)}, u32[]{:S(2)}) %collective-permute-start) | collective-permute-done | bytes 524320 | tf_op jit(solution)/shard_map/ppermute | solution.py:446
  16.1 0.7 collective-permute-done.1.v_other
  16.8 0.0 copy-done
  16.8 0.0 copy-done.1
  16.8 1.9 %prepare.1 = (bf16[2,4,256,256]{3,2,1,0:T(8,128)(2,1)S(1)}, bf16[2,4,256,256]{3,2,1,0:T(8,128)(2,1)S(1)}, bf16[2,4,16,256]{3,2,1,0:T(8,128)(2,1)S(1)}, f32[2,8,256]{2,1,0:T(8,128)S(1)}) custom-call(s32[1,128]{1,0:T(1,128)S(1)} %bitcast.6, s32[1,128]{1,0:T(1,128)S(1)} %bitcast.8, bf16[1024,256]{1,0:T(8,128)(2,1)} %bitcast.10, bf16[1024,256]{1,0:T(8,128)(2,1)} %bitcast.12, ...), custom_call_target="tpu_custom_call" | custom-call | tf_op jit(solution)/shard_map/prepare/pallas_call | solution.py:430
  18.7 14.1 %all-to-all-done.recv_ref = bf16[64,32,256]{2,1,0:T(8,128)(2,1)S(1)} async-done(((bf16[64,32,256]{2,1,0:T(8,128)(2,1)}), bf16[64,32,256]{2,1,0:T(8,128)(2,1)S(1)}, u32[]{:S(2)}, u32[]{:S(2)}) %all-to-all-start) | async-done | bytes 1048608 | tf_op jit(solution)/shard_map/all_to_all | solution.py:467
  32.8 35.6 %attention.1 = bf16[64,72,128]{2,1,0:T(8,128)(2,1)S(1)} custom-call(s32[1,128]{1,0:T(1,128)S(1)} %bitcast.7, s32[1,128]{1,0:T(1,128)S(1)} %bitcast.9, bf16[64,32,256]{2,1,0:T(8,128)(2,1)S(1)} %all-to-all-done.recv_ref, bf16[2,4,256,256]{3,2,1,0:T(8,128)(2,1)S(1)} %get-tuple-element.13.k_ref, bf16[2,4,256,256]{3,2,1,0:T(8,128)(2,1)S(1)} %get-tuple-element.14.vt_ref, ...), custom_call_target="tpu_custom_call" | custom-call | tf_op jit(solution)/shard_map/attention/pallas_call | solution.py:430
  68.4 38.1 %all_to_all.10.ret_ref = bf16[64,72,128]{2,1,0:T(8,128)(2,1)S(1)} all-to-all(bf16[64,72,128]{2,1,0:T(8,128)(2,1)S(1)} %attention.1), channel_id=1, replica_groups=mesh['y'=4,'core'=2,'col'=16] {'y','col'}, dimensions={0} | all-to-all | bytes 2359296 | tf_op jit(solution)/shard_map/all_to_all | solution.py:493
  106.5 1.9 %combine.1 = bf16[4,128,256]{2,1,0:T(8,128)(2,1)} custom-call(f32[8,128]{1,0:T(8,128)S(1)} %get-tuple-element.11.pos_ref, bf16[64,72,128]{2,1,0:T(8,128)(2,1)S(1)} %all_to_all.10.ret_ref), custom_call_target="tpu_custom_call" | custom-call | tf_op jit(solution)/shard_map/combine/pallas_call | solution.py:494
Async XLA Ops:
  0.0 14.1 %copy-start.2 = (bf16[1,1024,256]{2,1,0:T(8,128)(2,1)S(1)}, bf16[1,1024,256]{2,1,0:T(8,128)(2,1)}, u32[]{:S(2)}) copy-start(bf16[1,1024,256]{2,1,0:T(8,128)(2,1)} %param.8) | copy-start | bytes 1572868
  0.0 14.2 %copy-start.3 = (bf16[1,1024,256]{2,1,0:T(8,128)(2,1)S(1)}, bf16[1,1024,256]{2,1,0:T(8,128)(2,1)}, u32[]{:S(2)}) copy-start(bf16[1,1024,256]{2,1,0:T(8,128)(2,1)} %param.9) | copy-start | bytes 1572868
  0.0 16.8 %copy-start = (s32[128]{0:T(128)S(1)}, s32[128]{0:T(128)}, u32[]{:S(2)}) copy-start(s32[128]{0:T(128)} %param.10) | copy-start | bytes 1540
  0.0 16.8 %copy-start.1 = (s32[128]{0:T(128)S(1)}, s32[128]{0:T(128)}, u32[]{:S(2)}) copy-start(s32[128]{0:T(128)} %param.11) | copy-start | bytes 1540
  2.5 30.3 %all-to-all-start = ((bf16[64,32,256]{2,1,0:T(8,128)(2,1)}), bf16[64,32,256]{2,1,0:T(8,128)(2,1)S(1)}, u32[]{:S(2)}, u32[]{:S(2)}) async-start(bf16[64,32,256]{2,1,0:T(8,128)(2,1)} %get-tuple-element.12), calls=%async_computation | async-start | bytes 2097152 | tf_op jit(solution)/shard_map/all_to_all | solution.py:467
  14.1 2.0 %collective-permute-start = (bf16[1024,256]{1,0:T(8,128)(2,1)S(1)}, bf16[1024,256]{1,0:T(8,128)(2,1)S(1)}, u32[]{:S(2)}, u32[]{:S(2)}) collective-permute-start(bf16[1024,256]{1,0:T(8,128)(2,1)S(1)} %bitcast.11), channel_id=1, source_target_pairs={{0,16},{16,0},{1,17},{17,1},{2,18},{18,2},{3,19},{19,3},{4,20},{20... | collective-permute-start | bytes 1572872 | tf_op jit(solution)/shard_map/ppermute | solution.py:446
  14.2 2.6 %collective-permute-start.1 = (bf16[1024,256]{1,0:T(8,128)(2,1)S(1)}, bf16[1024,256]{1,0:T(8,128)(2,1)S(1)}, u32[]{:S(2)}, u32[]{:S(2)}) collective-permute-start(bf16[1024,256]{1,0:T(8,128)(2,1)S(1)} %bitcast.13), channel_id=1, source_target_pairs={{0,16},{16,0},{1,17},{17,1},{2,18},{18,2},{3,19},{19,3},{4,20},{20... | collective-permute-start | bytes 1572872 | tf_op jit(solution)/shard_map/ppermute | solution.py:447
